TPU v7x, 128 devices: a whole 4x4x4 slice. The times are simulated.
128 devices in a mesh: dp: 8 (over z, core), tensor: 16 (over y, x).
Axes of the slice: x: 4, y: 4, z: 4, core: 2. Of those that a mesh axis runs over, the one named last changes fastest.
Arguments:
- residues: bfloat16 [4096, 1024], P('dp'), may hold values from -40 to 40
- block_protein: int32 [32], P('dp'), may hold values from 0 to 31, as said below
- protein_length: int32 [32], replicated, may hold values from 0 to 256, as said below
- decoder_group: int32 [32], replicated, may hold values from 0 to 7, as said below
- enc_gain: float32 [1024], replicated, may hold values from 0.1 to 1.9
- enc_query: bfloat16 [1024, 16384], P(None, 'tensor'), may hold values from -2 to 2
- enc_key: bfloat16 [1024, 16384], P(None, 'tensor'), may hold values from -2 to 2
- enc_value: bfloat16 [1024, 16384], P(None, 'tensor'), may hold values from -0.1875 to 0.1875
- enc_out: bfloat16 [16384, 1024], P('tensor'), may hold values from -0.1875 to 0.1875
- decoder_states: bfloat16 [3072, 1024], P('dp'), may hold values from -40 to 40
- query_protein: int32 [3072], P('dp'), may hold values from 0 to 31, as said below
- dec_gain: float32 [1024], replicated, may hold values from 0.1 to 1.9
- final_gain: float32 [1024], replicated, may hold values from 0.1 to 1.9
- cross_query: bfloat16 [1024, 16384], P(None, 'tensor'), may hold values from -2 to 2
- cross_key: bfloat16 [1024, 16384], P(None, 'tensor'), may hold values from -2 to 2
- cross_value: bfloat16 [1024, 16384], P(None, 'tensor'), may hold values from -0.1875 to 0.1875
- cross_out: bfloat16 [16384, 1024], P('tensor'), may hold values from -0.1875 to 0.1875
Outputs:
- encoded: bfloat16 [4096, 1024], P('dp', 'tensor')
- decoded: bfloat16 [3072, 1024], P(('dp', 'tensor'))
Inputs may be any that keep to these rules, and one draw needn't show every extreme that they name: `block_protein`: block b of dp group d names a protein id from d * 4 to (d + 1) * 4 - 1; the blocks of one protein are consecutive and the ids rise along a group's blocks. `protein_length`: A protein of n blocks has a length from (n - 1) * 128 + 1 to n * 128; an id that no block names has length 0; no protein spans more than 2 blocks. `decoder_group`: at most 2 blocks of one dp group belong to proteins of one decoder group, and in every draw some decoder group gets exactly 2 blocks from every dp group; every decoder group owns a protein of positive length. `query_protein`: query row i names a protein of positive length whose decoder group is i // 384.
All inputs are finite; a program needn't handle non-finite values.
Results may differ from a plain program's by a relative error of at most 0.017.
Values may be sent and summed in bfloat16 or wider, within the bound.
No kernel may reach another device: no remote copies, remote signals or barrier semaphores. Data moves between devices by JAX's collectives and lax.ppermute only.
A program may use at most 128 MiB of HBM per device.

v0:
```python
import jax
import jax.numpy as jnp
from jax import lax
from jax.sharding import PartitionSpec as P

HEAD_DIM = 128
BLOCK = 128
EPSILON = 1e-06
MASKED = -1000000000.0


def split_up(x, dim, size):
    before, after = (x.shape[:dim], x.shape[dim + 1 :])
    return jnp.moveaxis(x.reshape(*before, size, -1, *after), dim, 0)


def sent_and_summed(x, axis, dim):
    blocks = split_up(x, dim, lax.axis_size(axis))
    arrived = lax.all_to_all(blocks, axis, split_axis=0, concat_axis=0, tiled=True)
    return arrived.sum(axis=0)


def summed_on_arrival(x, axis, dim):
    blocks = split_up(x, dim, lax.axis_size(axis))
    arrived = lax.all_to_all(blocks, axis, split_axis=0, concat_axis=0, tiled=True)
    return arrived.astype(jnp.float32).sum(axis=0)


def row_scale(matrix):
    values = matrix.astype(jnp.float32)
    return lax.rsqrt(jnp.mean(values * values, axis=1, keepdims=True) + EPSILON)


def table_lookup(indices, table):
    match = indices[:, None] == jnp.arange(table.shape[0], dtype=jnp.int32)[None, :]
    return jnp.sum(jnp.where(match, table[None, :], 0), axis=1)


def attend(queries, keys, values, allowed):
    count = queries.shape[0]
    heads = queries.shape[1] // HEAD_DIM
    query_heads = queries.reshape(count, heads, HEAD_DIM)
    key_heads = keys.reshape(keys.shape[0], heads, HEAD_DIM)
    value_heads = values.reshape(values.shape[0], heads, HEAD_DIM)
    scores = jnp.einsum(
        "qhd,khd->hqk", query_heads, key_heads, preferred_element_type=jnp.float32
    ) * HEAD_DIM ** (-0.5)
    scores = jnp.where(allowed[None], scores, MASKED)
    top = jnp.max(scores, axis=2, keepdims=True)
    expo = jnp.exp(scores - top)
    total = jnp.sum(expo, axis=2)
    weights = expo.astype(jnp.bfloat16)
    context = jnp.einsum("hqk,khd->qhd", weights, value_heads, preferred_element_type=jnp.float32)
    context = context / jnp.transpose(total)[:, :, None]
    return context.reshape(count, heads * HEAD_DIM).astype(jnp.bfloat16)


def body(
    residues,
    block_protein,
    protein_length,
    decoder_group,
    enc_gain,
    enc_query,
    enc_key,
    enc_value,
    enc_out,
    decoder_states,
    query_protein,
    dec_gain,
    final_gain,
    cross_query,
    cross_key,
    cross_value,
    cross_out,
):
    groups = lax.axis_size("dp")
    tensor_count = lax.axis_size("tensor")
    tensor_index = lax.axis_index("tensor")
    tok_rows = residues.shape[0]
    width = residues.shape[1]
    blocks = block_protein.shape[0]
    slots = blocks // 2
    order = jnp.arange(blocks, dtype=jnp.int32)
    same = block_protein[:, None] == block_protein[None, :]
    offset = jnp.sum(same & (order[None, :] < order[:, None]), axis=1)
    live = jnp.clip(table_lookup(block_protein, protein_length) - offset * BLOCK, 0, BLOCK)
    dest = table_lookup(block_protein, decoder_group)
    position = jnp.arange(BLOCK, dtype=jnp.int32)
    token_protein = jnp.broadcast_to(block_protein[:, None], (blocks, BLOCK)).reshape(tok_rows)
    token_valid = (position[None, :] < live[:, None]).reshape(tok_rows)
    normed = (residues.astype(jnp.float32) * row_scale(residues) * enc_gain[None, :]).astype(
        jnp.bfloat16
    )
    enc_queries = jnp.dot(normed, enc_query, preferred_element_type=jnp.float32).astype(
        jnp.bfloat16
    )
    enc_keys = jnp.dot(normed, enc_key, preferred_element_type=jnp.float32).astype(jnp.bfloat16)
    enc_values = jnp.dot(normed, enc_value, preferred_element_type=jnp.float32).astype(jnp.bfloat16)
    row_block = min(tok_rows, 512)
    block_count = tok_rows // row_block

    def encode_block(item):
        block_queries, block_owner = item
        permit = (block_owner[:, None] == token_protein[None, :]) & token_valid[None, :]
        return attend(block_queries, enc_keys, enc_values, permit)

    context = lax.map(
        encode_block,
        (
            enc_queries.reshape(block_count, row_block, -1),
            token_protein.reshape(block_count, row_block),
        ),
    )
    context = context.reshape(tok_rows, -1)
    partial_value = jnp.dot(context, enc_out, preferred_element_type=jnp.float32)
    slice_width = width // tensor_count
    column_start = tensor_index * slice_width
    same_dest = dest[:, None] == dest[None, :]
    rank = jnp.sum(same_dest & (order[None, :] < order[:, None]), axis=1)
    place = dest * slots + rank
    target = jnp.arange(groups * slots, dtype=jnp.int32)
    chosen = target[:, None] == place[None, :]
    occupied = jnp.any(chosen, axis=1)
    send_ids = jnp.where(
        occupied, jnp.sum(jnp.where(chosen, block_protein[None, :], 0), axis=1), -1
    )
    send_live = jnp.sum(jnp.where(chosen, live[None, :], 0), axis=1)
    send_meta = jnp.stack([send_ids, send_live], axis=-1).reshape(groups, slots, 2)
    shares = sent_and_summed(partial_value, "tensor", 1)
    own_columns = lax.dynamic_slice_in_dim(residues, column_start, slice_width, 1)
    encoded = (own_columns.astype(jnp.float32) + shares).astype(jnp.bfloat16)
    features = encoded.shape[1]
    stacked = encoded.reshape(blocks, BLOCK * features)
    placed = jnp.dot(
        chosen.astype(jnp.bfloat16), stacked, preferred_element_type=jnp.float32
    ).astype(jnp.bfloat16)
    slice_grid = lax.all_to_all(
        placed.reshape(groups, slots, BLOCK, features),
        "dp",
        split_axis=0,
        concat_axis=0,
        tiled=True,
    )
    meta = lax.all_to_all(send_meta, "dp", split_axis=0, concat_axis=0, tiled=True)
    flat = slice_grid.reshape(-1, slice_width)
    inner = cross_key.shape[1]
    values32 = lax.all_gather(flat, "tensor", axis=1, tiled=True).astype(jnp.float32)
    scaled = (values32 * final_gain[None, :]).astype(jnp.bfloat16)
    key_sum = jnp.dot(scaled, cross_key, preferred_element_type=jnp.float32)
    value_sum = jnp.dot(scaled, cross_value, preferred_element_type=jnp.float32)
    squares = jnp.sum(values32 * values32, axis=1, keepdims=True)
    key_sum, value_sum, squares = (key_sum, value_sum, squares)
    key_scale = lax.rsqrt(squares / width + EPSILON)
    grid_shape = (groups, slots, BLOCK, inner)
    key_grid = (key_sum * key_scale).astype(jnp.bfloat16).reshape(grid_shape)
    value_grid = (value_sum * key_scale).astype(jnp.bfloat16).reshape(grid_shape)
    key_ids = meta[:, :, 0]
    key_live = meta[:, :, 1]
    key_valid = position[None, None, :] < key_live[:, :, None]
    query_rows = decoder_states.shape[0]
    dec_normed = (
        decoder_states.astype(jnp.float32) * row_scale(decoder_states) * dec_gain[None, :]
    ).astype(jnp.bfloat16)
    cross_queries = jnp.dot(dec_normed, cross_query, preferred_element_type=jnp.float32).astype(
        jnp.bfloat16
    )
    allowed = (query_protein[:, None, None, None] == key_ids[None, :, :, None]) & key_valid[None]
    slot_total = groups * slots
    inner_width = key_grid.shape[3]
    cross_context = attend(
        cross_queries,
        key_grid.reshape(slot_total * BLOCK, inner_width),
        value_grid.reshape(slot_total * BLOCK, inner_width),
        allowed.reshape(query_rows, slot_total * BLOCK),
    )
    share_rows = query_rows // tensor_count
    mixed = summed_on_arrival(
        jnp.dot(cross_context, cross_out, preferred_element_type=jnp.float32).astype(jnp.bfloat16),
        "tensor",
        0,
    )
    own_rows = lax.dynamic_slice_in_dim(decoder_states, tensor_index * share_rows, share_rows, 0)
    decoded = (own_rows.astype(jnp.float32) + mixed).astype(jnp.bfloat16)
    return (encoded, decoded)


def solution(mesh):
    in_specs = (
        P("dp", None),
        P("dp"),
        P(),
        P(),
        P(),
        P(None, "tensor"),
        P(None, "tensor"),
        P(None, "tensor"),
        P("tensor", None),
        P("dp", None),
        P("dp"),
        P(),
        P(),
        P(None, "tensor"),
        P(None, "tensor"),
        P(None, "tensor"),
        P("tensor", None),
    )
    out_specs = (P("dp", "tensor"), P(("dp", "tensor"), None))
    return jax.shard_map(body, mesh=mesh, in_specs=in_specs, out_specs=out_specs, check_vma=False)
```

profile of v0, /device:TPU:0, one launch (start us, length us, event | category | flops | bytes accessed | tf_op | source)
XLA Modules:
  0.0 220.1 jit_solution(1068523723538875895)
XLA Ops:
  7.2 1.0 convert_reduce_fusion.2
  8.9 0.9 select_reduce_fusion.2
  10.1 1.5 fusion.17
  11.6 4.4 %fusion.31 = bf16[64,8,8,128]{3,2,1,0:T(8,128)(2,1)} fusion(bf16[1024,1024]{1,0:T(8,128)(2,1)} %param.22, bf16[512,1024]{1,0:T(8,128)(2,1)} %param.17, f32[1024]{0:T(1024)} %param.21, f32[512]{0:T(512)S(1)} %add_rsqrt_fusion.2), kind=kOutput, calls=%fused_computation.46 | convolution fusion | flops 1076363264 | bytes 4200448 | tf_op jit(solution)/shard_map/dot_general | solution.py:95
  16.0 2.3 %fusion.32 = bf16[64,8,8,128]{3,2,1,0:T(8,128)(2,1)} fusion(bf16[1024,1024]{1,0:T(8,128)(2,1)S(1)} %copy-done.11, bf16[512,1024]{1,0:T(8,128)(2,1)S(1)} %copy-done.6, f32[1024]{0:T(1024)S(1)} %copy-done.14, f32[512]{0:T(512)S(1)} %add_rsqrt_fusion.2), kind=kOutput, calls=%fused_computation.47 | convolution fusion | flops 1076363264 | bytes 4200448 | tf_op jit(solution)/shard_map/dot_general | solution.py:98
  18.3 2.3 %convolution_convert_fusion.3 = bf16[512,1024]{1,0:T(8,128)(2,1)} fusion(bf16[1024,1024]{1,0:T(8,128)(2,1)S(1)} %copy-done.12, bf16[512,1024]{1,0:T(8,128)(2,1)S(1)} %copy-done.6, f32[1024]{0:T(1024)S(1)} %copy-done.14, f32[512]{0:T(512)S(1)} %add_rsqrt_fusion.2), kind=kOutput, calls=%fused_computation.43 | convolution fusion | flops 1076363264 | bytes 4200448 | tf_op jit(solution)/shard_map/dot_general | solution.py:99
  20.6 2.3 %copy.107 = bf16[512,1024]{0,1:T(8,128)(2,1)} copy(bf16[512,1024]{1,0:T(8,128)(2,1)} %convolution_convert_fusion.3) | data formatting | bytes 2097152 | tf_op jit(solution)/shard_map/while/body/eval_jaxpr/reshape | solution.py:44
  22.9 4.0 %copy.91 = bf16[1024,1024]{0,1:T(8,128)(2,1)} copy(bf16[1024,1024]{1,0:T(8,128)(2,1)} %param.25) | data formatting | bytes 4194304 | tf_op args[8]
  27.1 3.2 %fusion.8 = (f32[8,512]{1,0:T(8,128)S(1)}, f32[8,512,512]{1,2,0:T(8,128)S(1)}) fusion(pred[512,512]{0,1:T(8,128)(4,1)S(1)} %compare_and_fusion, bf16[64,8,8,128]{3,2,1,0:T(8,128)(2,1)} %fusion.32, bf16[64,8,8,128]{3,2,1,0:T(8,128)(2,1)} %fusion.31), kind=kOutput, calls=%fused_computation.16 | convolution fusion | flops 543158272 | bytes 10764288 | tf_op jit(solution)/shard_map/while/body/eval_jaxpr/qhd,khd->hqk/dot_general | solution.py:45
  30.3 1.7 fusion.9
  32.1 2.6 %fusion.20 = bf16[512,8,128]{0,2,1:T(8,128)(2,1)S(1)} fusion(bf16[512,8,128]{0,2,1:T(8,128)(2,1)S(1)} %bitcast.70, f32[8,512,512]{1,2,0:T(8,128)S(1)} %get-tuple-element.33, f32[8,512]{1,0:T(8,128)S(1)} %get-tuple-element.32, pred[512,512]{0,1:T(8,128)(4,1)S(1)} %compare_and_fusion, f32[512,8]{0,1:T(8,128)S(1)} %bitcast.72), kind=kOutput, calls=%fused_computation.31 | convolution fusion | flops 546308096 | bytes 10780672 | tf_op jit(solution)/shard_map/while/body/eval_jaxpr/hqk,khd->qhd/dot_general | solution.py:53
  34.7 2.5 %convolution_bitcast_fusion = f32[16,512,64]{1,2,0:T(8,128)} fusion(bf16[512,1024,1]{0,1,2:T(8,128)(2,1)S(1)} %bitcast.77, bf16[16,64,1024]{2,1,0:T(8,128)(2,1)S(1)} %bitcast.69), kind=kOutput, calls=%fused_computation.34 | convolution fusion | flops 1073741824 | bytes 5242880 | tf_op jit(solution)/shard_map/dot_general | solution.py:116
  37.2 7.2 %all-to-all-start = ((f32[16,512,64]{1,2,0:T(8,128)}), f32[16,512,64]{1,2,0:T(8,128)}, u32[]{:S(2)}, u32[]{:S(2)}) async-start(f32[16,512,64]{1,2,0:T(8,128)} %convolution_bitcast_fusion), calls=%async_computation | async-start | bytes 4194304 | tf_op jit(solution)/shard_map/all_to_all | solution.py:19
  44.7 31.5 %all-to-all-done = f32[16,512,64]{1,2,0:T(8,128)} async-done(((f32[16,512,64]{1,2,0:T(8,128)}), f32[16,512,64]{1,2,0:T(8,128)}, u32[]{:S(2)}, u32[]{:S(2)}) %all-to-all-start) | async-done | bytes 2097184 | tf_op jit(solution)/shard_map/all_to_all | solution.py:19
  76.2 1.8 reduce_sum.122
  79.4 12.7 %all_to_all.20 = bf16[8,2,128,64]{2,3,1,0:T(8,128)(2,1)S(1)} all-to-all(bf16[8,2,128,64]{2,3,1,0:T(8,128)(2,1)S(1)} %copy.94), channel_id=1, replica_groups=mesh['dp'=8,'tensor'=16] {'dp'}, dimensions={0} | all-to-all | bytes 524288 | tf_op jit(solution)/shard_map/all_to_all | solution.py:138
  94.3 3.5 %all-to-all-start.2 = ((s32[8,2,2]{1,2,0:T(2,128)}), s32[8,2,2]{1,2,0:T(2,128)S(1)}, u32[]{:S(2)}, u32[]{:S(2)}) async-start(s32[8,2,2]{1,2,0:T(2,128)} %copy.96), calls=%async_computation.2 | async-start | bytes 16384 | tf_op jit(solution)/shard_map/all_to_all | solution.py:145
  97.8 1.4 fusion.25
  99.2 3.9 %fusion.33 = bf16[48,8,8,128]{3,2,1,0:T(8,128)(2,1)} fusion(bf16[1024,1024]{1,0:T(8,128)(2,1)} %param.30, bf16[384,1024]{1,0:T(8,128)(2,1)} %param.26, f32[1024]{0:T(1024)S(1)} %copy-done.15, f32[384]{0:T(512)S(1)} %add_rsqrt_fusion.1), kind=kOutput, calls=%fused_computation.48 | convolution fusion | flops 807272448 | bytes 3675648 | tf_op jit(solution)/shard_map/dot_general | solution.py:165
  103.3 1.3 bitcast_and_fusion
  104.6 2.2 copy.101
  106.8 33.9 %all-gather.2.cloned.1.call-done = bf16[2048,1024]{0,1:T(8,128)(2,1)} async-done(((bf16[2048,64]{0,1:T(8,128)(2,1)}), bf16[2048,1024]{0,1:T(8,128)(2,1)}) %all-gather.2.cloned.1.call-update) | async-done | bytes 4194320 | tf_op jit(solution)/shard_map/all_gather | solution.py:148
  140.7 3.2 %fusion.7 = f32[2048]{0:T(1024)S(1)} fusion(bf16[2048,1024]{0,1:T(8,128)(2,1)} %all-gather.2.cloned.1.call-done), kind=kLoop, calls=%fused_computation.11 | loop fusion | flops 6289408 | bytes 4202496 | tf_op jit(solution)/shard_map/reduce_sum | solution.py:152
  144.1 5.6 %multiply_convert_fusion = bf16[2048,1024]{0,1:T(8,128)(2,1)S(1)} fusion(bf16[1024,1024]{1,0:T(8,128)(2,1)S(1)} %copy-done, f32[2048]{0:T(1024)S(1)} %add_rsqrt_fusion, bf16[2048,1024]{0,1:T(8,128)(2,1)S(1)} %copy-done.2, f32[1024]{0:T(1024)S(1)} %copy-done.16), kind=kOutput, calls=%fused_computation.12 | convolution fusion | flops 4305453056 | bytes 10498048 | tf_op jit(solution)/shard_map/dot_general | solution.py:150
  149.8 10.9 %fusion = (f32[8,384]{1,0:T(8,128)S(1)}, f32[8,384,2048]{2,1,0:T(8,128)}) fusion(pred[384,2048]{1,0:T(8,128)(4,1)S(1)} %copy.101, bf16[2048,8,128]{0,2,1:T(8,128)(2,1)S(1)} %bitcast.68, bf16[48,8,8,128]{3,2,1,0:T(8,128)(2,1)S(1)} %copy-done.5), kind=kOutput, calls=%fused_computation.2 | convolution fusion | flops 1629484032 | bytes 30945280 | tf_op jit(solution)/shard_map/qhd,khd->hqk/dot_general | solution.py:45
  160.7 11.7 %fusion.1 = f32[8,384]{1,0:T(8,128)S(1)} fusion(f32[8,384,2048]{2,1,0:T(8,128)} %get-tuple-element.35, f32[8,384]{1,0:T(8,128)S(1)} %get-tuple-element.34, pred[384,2048]{1,0:T(8,128)(4,1)S(1)} %copy.101), kind=kLoop, calls=%fused_computation.3 | loop fusion | flops 25162752 | bytes 25976832 | tf_op jit(solution)/shard_map/reduce_sum | solution.py:51
  172.4 5.6 %multiply_convert_fusion.1 = bf16[2048,1024]{0,1:T(8,128)(2,1)S(1)} fusion(bf16[1024,1024]{1,0:T(8,128)(2,1)S(1)} %copy-done.13, f32[2048]{0:T(1024)S(1)} %add_rsqrt_fusion, bf16[2048,1024]{0,1:T(8,128)(2,1)S(1)} %copy-done.2, f32[1024]{0:T(1024)S(1)} %copy-done.16), kind=kOutput, calls=%fused_computation.13 | convolution fusion | flops 4305453056 | bytes 10498048 | tf_op jit(solution)/shard_map/dot_general | solution.py:151
  178.1 12.2 %fusion.28 = bf16[384,8,128]{0,2,1:T(8,128)(2,1)S(1)} fusion(bf16[2048,8,128]{0,2,1:T(8,128)(2,1)S(1)} %bitcast.76, f32[8,384,2048]{2,1,0:T(8,128)} %get-tuple-element.35, f32[8,384]{1,0:T(8,128)S(1)} %get-tuple-element.34, pred[384,2048]{1,0:T(8,128)(4,1)S(1)} %copy.101, f32[384,8]{0,1:T(8,128)S(1)} %bitcast.75), kind=kOutput, calls=%fused_computation.39 | convolution fusion | flops 1636564992 | bytes 30957568 | tf_op jit(solution)/shard_map/hqk,khd->qhd/dot_general | solution.py:53
  190.3 1.9 convolution_convert_fusion.4
  192.1 5.3 %all-to-all-start.3 = ((bf16[16,24,1024]{2,1,0:T(8,128)(2,1)}), bf16[16,24,1024]{2,1,0:T(8,128)(2,1)S(1)}, u32[]{:S(2)}, u32[]{:S(2)}) async-start(bf16[16,24,1024]{2,1,0:T(8,128)(2,1)} %bitcast.18), calls=%async_computation.3 | async-start | bytes 1572864 | tf_op jit(solution)/shard_map/all_to_all | solution.py:25
  197.4 14.3 %all-to-all-done.3 = bf16[16,24,1024]{2,1,0:T(8,128)(2,1)S(1)} async-done(((bf16[16,24,1024]{2,1,0:T(8,128)(2,1)}), bf16[16,24,1024]{2,1,0:T(8,128)(2,1)S(1)}, u32[]{:S(2)}, u32[]{:S(2)}) %all-to-all-start.3) | async-done | bytes 786464 | tf_op jit(solution)/shard_map/all_to_all | solution.py:25
  211.8 1.4 add_convert_fusion.1
  (67 shorter events, 5.6 us)
Async XLA Ops:
  7.2 136.7 %copy-start = (bf16[1024,1024]{1,0:T(8,128)(2,1)S(1)}, bf16[1024,1024]{1,0:T(8,128)(2,1)}, u32[]{:S(2)}) copy-start(bf16[1024,1024]{1,0:T(8,128)(2,1)} %param.31) | copy-start | bytes 6291460
  11.6 4.4 %copy-start.6 = (bf16[512,1024]{1,0:T(8,128)(2,1)S(1)}, bf16[512,1024]{1,0:T(8,128)(2,1)}, u32[]{:S(2)}) copy-start(bf16[512,1024]{1,0:T(8,128)(2,1)} %param.17) | copy-start | bytes 3145732
  11.6 4.4 %copy-start.11 = (bf16[1024,1024]{1,0:T(8,128)(2,1)S(1)}, bf16[1024,1024]{1,0:T(8,128)(2,1)}, u32[]{:S(2)}) copy-start(bf16[1024,1024]{1,0:T(8,128)(2,1)} %param.23) | copy-start | bytes 6291460
  11.6 4.4 %copy-start.14 = (f32[1024]{0:T(1024)S(1)}, f32[1024]{0:T(1024)}, u32[]{:S(2)}) copy-start(f32[1024]{0:T(1024)} %param.21) | copy-start | bytes 12292
  16.0 2.3 %copy-start.12 = (bf16[1024,1024]{1,0:T(8,128)(2,1)S(1)}, bf16[1024,1024]{1,0:T(8,128)(2,1)}, u32[]{:S(2)}) copy-start(bf16[1024,1024]{1,0:T(8,128)(2,1)} %param.24) | copy-start | bytes 6291460
  30.3 1.8 copy-start.7
  32.1 2.6 %copy-start.4 = (bf16[1024,1024]{0,1:T(8,128)(2,1)S(1)}, bf16[1024,1024]{0,1:T(8,128)(2,1)}, u32[]{:S(2)}) copy-start(bf16[1024,1024]{0,1:T(8,128)(2,1)} %copy.91) | copy-start | bytes 6291460
  37.2 39.0 %all-to-all-start = ((f32[16,512,64]{1,2,0:T(8,128)}), f32[16,512,64]{1,2,0:T(8,128)}, u32[]{:S(2)}, u32[]{:S(2)}) async-start(f32[16,512,64]{1,2,0:T(8,128)} %convolution_bitcast_fusion), calls=%async_computation | async-start | bytes 4194304 | tf_op jit(solution)/shard_map/all_to_all | solution.py:19
  44.4 49.0 %copy-start.9 = (s32[4]{0:T(128)S(1)}, s32[4]{0:T(128)}, u32[]{:S(2)}) copy-start(s32[4]{0:T(128)} %param.18) | copy-start | bytes 52
  44.4 54.8 %copy-start.15 = (f32[1024]{0:T(1024)S(1)}, f32[1024]{0:T(1024)}, u32[]{:S(2)}) copy-start(f32[1024]{0:T(1024)} %param.28) | copy-start | bytes 12292
  44.4 96.2 %all-gather.2.cloned.1.call-start = ((), (), s32[]{:S(2)}) async-start(), calls=%async_computation.4 | async-start | bytes 4456448 | tf_op jit(solution)/shard_map/all_gather | solution.py:148
  78.0 25.0 %copy-start.8 = (bf16[512,64]{0,1:T(8,128)(2,1)}, bf16[512,64]{0,1:T(8,128)(2,1)S(1)}, u32[]{:S(2)}) copy-start(bf16[512,64]{0,1:T(8,128)(2,1)S(1)} %add_convert_fusion) | copy-start | bytes 196612
  92.4 10.8 %copy-start.10 = (s32[384]{0:T(512)S(1)}, s32[384]{0:T(512)}, u32[]{:S(2)}) copy-start(s32[384]{0:T(512)} %param.27) | copy-start | bytes 4612
  94.3 8.8 %all-to-all-start.2 = ((s32[8,2,2]{1,2,0:T(2,128)}), s32[8,2,2]{1,2,0:T(2,128)S(1)}, u32[]{:S(2)}, u32[]{:S(2)}) async-start(s32[8,2,2]{1,2,0:T(2,128)} %copy.96), calls=%async_computation.2 | async-start | bytes 16384 | tf_op jit(solution)/shard_map/all_to_all | solution.py:145
  103.1 40.9 %copy-start.16 = (f32[1024]{0:T(1024)S(1)}, f32[1024]{0:T(1024)}, u32[]{:S(2)}) copy-start(f32[1024]{0:T(1024)} %param.29) | copy-start | bytes 12292
  140.7 3.4 %copy-start.2 = (bf16[2048,1024]{0,1:T(8,128)(2,1)S(1)}, bf16[2048,1024]{0,1:T(8,128)(2,1)}, u32[]{:S(2)}) copy-start(bf16[2048,1024]{0,1:T(8,128)(2,1)} %all-gather.2.cloned.1.call-done) | copy-start | bytes 12582916
  144.1 5.6 %copy-start.5 = (bf16[48,8,8,128]{3,2,1,0:T(8,128)(2,1)S(1)}, bf16[48,8,8,128]{3,2,1,0:T(8,128)(2,1)}, u32[]{:S(2)}) copy-start(bf16[48,8,8,128]{3,2,1,0:T(8,128)(2,1)} %fusion.33) | copy-start | bytes 2359300
  160.7 11.7 %copy-start.13 = (bf16[1024,1024]{1,0:T(8,128)(2,1)S(1)}, bf16[1024,1024]{1,0:T(8,128)(2,1)}, u32[]{:S(2)}) copy-start(bf16[1024,1024]{1,0:T(8,128)(2,1)} %param.32) | copy-start | bytes 6291460
  178.0 12.2 %copy-start.3 = (bf16[1024,1024]{1,0:T(8,128)(2,1)S(1)}, bf16[1024,1024]{1,0:T(8,128)(2,1)}, u32[]{:S(2)}) copy-start(bf16[1024,1024]{1,0:T(8,128)(2,1)} %param.33) | copy-start | bytes 6291460
  178.1 35.2 %copy-start.1 = (bf16[1024,1024]{1,0:T(8,128)(2,1)S(1)}, bf16[1024,1024]{1,0:T(8,128)(2,1)}, u32[]{:S(2)}) copy-start(bf16[1024,1024]{1,0:T(8,128)(2,1)} %param.31) | copy-start | bytes 6291460
  192.1 19.6 %all-to-all-start.3 = ((bf16[16,24,1024]{2,1,0:T(8,128)(2,1)}), bf16[16,24,1024]{2,1,0:T(8,128)(2,1)S(1)}, u32[]{:S(2)}, u32[]{:S(2)}) async-start(bf16[16,24,1024]{2,1,0:T(8,128)(2,1)} %bitcast.18), calls=%async_computation.3 | async-start | bytes 1572864 | tf_op jit(solution)/shard_map/all_to_all | solution.py:25
Sparse Core Ops, SparseCore 0:
  93.4 47.2 all-gather.1
where the time goes:
time: 221 us; the launch traced here: 220 us
  waiting for transfers between devices  79.8 us (36%)
  matrix products  57.7 us (26%)
  other arithmetic  27 us (12%)
  starting transfers between devices  16 us (7%)
  between operations  14.4 us (7%)
  blocking collectives  12.7 us (6%)
  local copies, waits for them, and re-layouts  12.6 us (6%)
    all_gather x1, waiting for transfers between devices, body(): lax.all_gather(flat, 'tensor', axis=1, tiled=True).astype(jnp.float32)  33.9 us
    all_to_all x1, waiting for transfers between devices, sent_and_summed(): lax.all_to_all(blocks, axis, split_axis=0, concat_axis=0, tiled=True)  31.5 us
    dot_general x2, matrix products, attend(): jnp.einsum('hqk,khd->qhd', weights, value_heads, preferred_element_type=j...  14.7 us
    all_to_all x1, waiting for transfers between devices, summed_on_arrival(): lax.all_to_all(blocks, axis, split_axis=0, concat_axis=0, tiled=True)  14.3 us
    dot_general x2, matrix products, attend(): jnp.einsum('qhd,khd->hqk', query_heads, key_heads, preferred_element_type...  14.1 us
    reduce_sum x2, other arithmetic, attend(): total = jnp.sum(expo, axis=2)  13.4 us
    all_to_all x1, blocking collectives, body(): lax.all_to_all(placed.reshape(groups, slots, BLOCK, features), 'dp', spli...  12.7 us
    all_to_all x1, starting transfers between devices, sent_and_summed(): lax.all_to_all(blocks, axis, split_axis=0, concat_axis=0, tiled=True)  7.19 us
  transfers between devices with their start and end apart: 4, of which 3 were waited for; matrix products, arithmetic and copies ran while one was open for 5% of the time, Pallas kernels for 0%

commit v1 on v0

--- a/solution.py
+++ b/solution.py
@@ -7,6 +7,15 @@
 BLOCK = 128
 EPSILON = 1e-06
 MASKED = -1000000000.0
+view_ports = lambda block_in, axis_name: jnp.concatenate(
+    lax.all_to_all(
+        jnp.stack([block_in] * lax.axis_size(axis_name), 0),
+        axis_name=axis_name,
+        split_axis=0,
+        concat_axis=0,
+    ),
+    1,
+)
 
 
 def split_up(x, dim, size):
@@ -145,7 +154,7 @@
     meta = lax.all_to_all(send_meta, "dp", split_axis=0, concat_axis=0, tiled=True)
     flat = slice_grid.reshape(-1, slice_width)
     inner = cross_key.shape[1]
-    values32 = lax.all_gather(flat, "tensor", axis=1, tiled=True).astype(jnp.float32)
+    values32 = view_ports(flat, "tensor").astype(jnp.float32)
     scaled = (values32 * final_gain[None, :]).astype(jnp.bfloat16)
     key_sum = jnp.dot(scaled, cross_key, preferred_element_type=jnp.float32)
     value_sum = jnp.dot(scaled, cross_value, preferred_element_type=jnp.float32)

time: 221 us -> 240 us (1.086)
  waiting for transfers between devices: 79.8 us -> 112 us
  between operations: 14.4 us -> 1.01 us
  blocking collectives: 12.7 us -> 0 us
  starting transfers between devices: 16 us -> 25.6 us
    all_to_all x0 -> x2, waiting for transfers between devices: none -> 62.7 us  [the longest x1 56 us: lax.all_to_all(jnp.stack([block_in] * lax.axis_size(axis_name), 0), axis_...]
    all_gather x1 -> x0, waiting for transfers between devices: 33.9 us -> none  [body(): lax.all_gather(flat, 'tensor', axis=1, tiled=True).astype(jnp.float32)]
    all_to_all x1 -> x0, blocking collectives: 12.7 us -> none  [body(): lax.all_to_all(placed.reshape(groups, slots, BLOCK, features), 'dp', spli...]
    all_to_all x0 -> x2, starting transfers between devices: none -> 9.97 us  [the longest x1 5.3 us: body(): lax.all_to_all(placed.reshape(groups, slots, BLOCK, features), 'dp', spli...]
    all_to_all x1, waiting for transfers between devices: 0.01 us -> 4.77 us  [body(): lax.all_to_all(send_meta, 'dp', split_axis=0, concat_axis=0, tiled=True)]
    convert_element_type x0 -> x1, other arithmetic: none -> 2.93 us  [body(): scaled = (values32 * final_gain[None, :]).astype(jnp.bfloat16)]
    another operation x0 -> x2, local copies, waits for them, and re-layouts: none -> 2.68 us  [jnp.stack([block_in] * lax.axis_size(axis_name), 0)]
  transfers between devices with their start and end apart: 4 -> 5, of which waited for: 3 -> 5; matrix products, arithmetic and copies ran while one was open for 5% -> 4% of each run, Pallas kernels for 0% -> 0%
where the time goes in v1:
time: 240 us; the launch traced here: 239 us
  waiting for transfers between devices  112 us (47%)
  matrix products  56.2 us (23%)
  other arithmetic  28.4 us (12%)
  starting transfers between devices  25.6 us (11%)
  local copies, waits for them, and re-layouts  14.9 us (6%)
    all_to_all x1, waiting for transfers between devices, lax.all_to_all(jnp.stack([block_in] * lax.axis_size(axis_name), 0), axis_...  56 us
    all_to_all x1, waiting for transfers between devices, sent_and_summed(): lax.all_to_all(blocks, axis, split_axis=0, concat_axis=0, tiled=True)  31.4 us
    dot_general x2, matrix products, attend(): jnp.einsum('hqk,khd->qhd', weights, value_heads, preferred_element_type=j...  14.6 us
    dot_general x2, matrix products, attend(): jnp.einsum('qhd,khd->hqk', query_heads, key_heads, preferred_element_type...  14.1 us
    all_to_all x1, waiting for transfers between devices, summed_on_arrival(): lax.all_to_all(blocks, axis, split_axis=0, concat_axis=0, tiled=True)  13.5 us
    reduce_sum x2, other arithmetic, attend(): total = jnp.sum(expo, axis=2)  13.3 us
    all_to_all x1, starting transfers between devices, sent_and_summed(): lax.all_to_all(blocks, axis, split_axis=0, concat_axis=0, tiled=True)  7.35 us
    all_to_all x1, waiting for transfers between devices, body(): lax.all_to_all(placed.reshape(groups, slots, BLOCK, features), 'dp', spli...  6.72 us
  transfers between devices with their start and end apart: 5, of which 5 were waited for; matrix products, arithmetic and copies ran while one was open for 4% of the time, Pallas kernels for 0%

profile of v1, /device:TPU:0, one launch (start us, length us, event | category | flops | bytes accessed | tf_op | source)
XLA Modules:
  0.0 238.6 jit_solution(3362723099648566507)
XLA Ops:
  3.5 1.5 fusion.16
  5.1 4.4 %fusion.28 = bf16[64,8,8,128]{3,2,1,0:T(8,128)(2,1)} fusion(bf16[1024,1024]{1,0:T(8,128)(2,1)} %param.22, bf16[512,1024]{1,0:T(8,128)(2,1)} %param.17, f32[1024]{0:T(1024)} %param.21, f32[512]{0:T(512)S(1)} %add_rsqrt_fusion.2), kind=kOutput, calls=%fused_computation.45 | convolution fusion | flops 1076363264 | bytes 4200448 | tf_op jit(solution)/shard_map/dot_general | solution.py:104
  9.5 2.3 fusion.29
  11.8 2.3 convolution_convert_fusion.3
  14.1 2.3 copy.108
  16.4 4.0 %copy.92 = bf16[1024,1024]{0,1:T(8,128)(2,1)} copy(bf16[1024,1024]{1,0:T(8,128)(2,1)} %param.25) | data formatting | bytes 4194304 | tf_op args[8]
  20.6 3.2 %fusion.7 = (f32[8,512]{1,0:T(8,128)S(1)}, f32[8,512,512]{1,2,0:T(8,128)S(1)}) fusion(pred[512,512]{0,1:T(8,128)(4,1)S(1)} %compare_and_fusion, bf16[64,8,8,128]{3,2,1,0:T(8,128)(2,1)} %fusion.29, bf16[64,8,8,128]{3,2,1,0:T(8,128)(2,1)} %fusion.28), kind=kOutput, calls=%fused_computation.15 | convolution fusion | flops 543158272 | bytes 10764288 | tf_op jit(solution)/shard_map/while/body/eval_jaxpr/qhd,khd->hqk/dot_general | solution.py:54
  23.8 1.7 fusion.8
  25.6 2.6 %fusion.19 = bf16[512,8,128]{0,2,1:T(8,128)(2,1)S(1)} fusion(bf16[512,8,128]{0,2,1:T(8,128)(2,1)S(1)} %bitcast.78, f32[8,512,512]{1,2,0:T(8,128)S(1)} %get-tuple-element.33, f32[8,512]{1,0:T(8,128)S(1)} %get-tuple-element.32, pred[512,512]{0,1:T(8,128)(4,1)S(1)} %compare_and_fusion, f32[512,8]{0,1:T(8,128)S(1)} %bitcast.80), kind=kOutput, calls=%fused_computation.30 | convolution fusion | flops 546308096 | bytes 10780672 | tf_op jit(solution)/shard_map/while/body/eval_jaxpr/hqk,khd->qhd/dot_general | solution.py:62
  28.1 2.5 %convolution_bitcast_fusion = f32[16,512,64]{1,2,0:T(8,128)} fusion(bf16[512,1024,1]{0,1,2:T(8,128)(2,1)S(1)} %bitcast.85, bf16[16,64,1024]{2,1,0:T(8,128)(2,1)S(1)} %bitcast.77), kind=kOutput, calls=%fused_computation.33 | convolution fusion | flops 1073741824 | bytes 5242880 | tf_op jit(solution)/shard_map/dot_general | solution.py:125
  30.7 7.3 %all-to-all-start = ((f32[16,512,64]{1,2,0:T(8,128)}), f32[16,512,64]{1,2,0:T(8,128)}, u32[]{:S(2)}, u32[]{:S(2)}) async-start(f32[16,512,64]{1,2,0:T(8,128)} %convolution_bitcast_fusion), calls=%async_computation | async-start | bytes 4194304 | tf_op jit(solution)/shard_map/all_to_all | solution.py:28
  38.4 31.4 %all-to-all-done = f32[16,512,64]{1,2,0:T(8,128)} async-done(((f32[16,512,64]{1,2,0:T(8,128)}), f32[16,512,64]{1,2,0:T(8,128)}, u32[]{:S(2)}, u32[]{:S(2)}) %all-to-all-start) | async-done | bytes 2097184 | tf_op jit(solution)/shard_map/all_to_all | solution.py:28
  69.9 1.8 reduce_sum.122
  73.7 5.3 %all-to-all-start.1 = ((bf16[8,2,128,64]{2,3,1,0:T(8,128)(2,1)}), bf16[8,2,128,64]{2,3,1,0:T(8,128)(2,1)S(1)}, u32[]{:S(2)}, u32[]{:S(2)}) async-start(bf16[8,2,128,64]{2,3,1,0:T(8,128)(2,1)} %copy.95), calls=%async_computation.1 | async-start | bytes 524288 | tf_op jit(solution)/shard_map/all_to_all | solution.py:147
  79.8 6.7 %all-to-all-done.1 = bf16[8,2,128,64]{2,3,1,0:T(8,128)(2,1)S(1)} async-done(((bf16[8,2,128,64]{2,3,1,0:T(8,128)(2,1)}), bf16[8,2,128,64]{2,3,1,0:T(8,128)(2,1)S(1)}, u32[]{:S(2)}, u32[]{:S(2)}) %all-to-all-start.1) | async-done | bytes 262176 | tf_op jit(solution)/shard_map/all_to_all | solution.py:147
  86.6 3.3 %all-to-all-start.3 = ((s32[8,2,2]{1,2,0:T(2,128)}), s32[8,2,2]{1,2,0:T(2,128)S(1)}, u32[]{:S(2)}, u32[]{:S(2)}) async-start(s32[8,2,2]{1,2,0:T(2,128)} %copy.97), calls=%async_computation.3 | async-start | bytes 16384 | tf_op jit(solution)/shard_map/all_to_all | solution.py:154
  90.4 4.8 %all-to-all-done.3 = s32[8,2,2]{1,2,0:T(2,128)S(1)} async-done(((s32[8,2,2]{1,2,0:T(2,128)}), s32[8,2,2]{1,2,0:T(2,128)S(1)}, u32[]{:S(2)}, u32[]{:S(2)}) %all-to-all-start.3) | async-done | bytes 160 | tf_op jit(solution)/shard_map/all_to_all | solution.py:154
  95.1 2.5 %stack.10 = bf16[16,2048,64]{1,2,0:T(8,128)(2,1)} broadcast(bf16[2048,64]{0,1:T(8,128)(2,1)S(1)} %stack_reshape.2), dimensions={1,2} | broadcast | bytes 4456448 | tf_op jit(solution)/shard_map/stack | solution.py:12
  97.6 4.7 %all-to-all-start.2 = ((bf16[16,2048,64]{1,2,0:T(8,128)(2,1)}), bf16[16,2048,64]{1,2,0:T(8,128)(2,1)}, u32[]{:S(2)}, u32[]{:S(2)}) async-start(bf16[16,2048,64]{1,2,0:T(8,128)(2,1)} %stack.10), calls=%async_computation.2 | async-start | bytes 8388608 | tf_op jit(solution)/shard_map/all_to_all | solution.py:11
  102.6 3.6 %fusion.30 = bf16[48,8,8,128]{3,2,1,0:T(8,128)(2,1)} fusion(bf16[1024,1024]{1,0:T(8,128)(2,1)} %param.30, bf16[384,1024]{1,0:T(8,128)(2,1)S(1)} %copy-done.7, f32[1024]{0:T(1024)S(1)} %copy-done.16, f32[384]{0:T(512)S(1)} %add_rsqrt_fusion.1), kind=kOutput, calls=%fused_computation.47 | convolution fusion | flops 807272448 | bytes 3675648 | tf_op jit(solution)/shard_map/dot_general | solution.py:174
  107.6 2.2 copy.102
  109.8 56.0 %all-to-all-done.2 = bf16[16,2048,64]{1,2,0:T(8,128)(2,1)} async-done(((bf16[16,2048,64]{1,2,0:T(8,128)(2,1)}), bf16[16,2048,64]{1,2,0:T(8,128)(2,1)}, u32[]{:S(2)}, u32[]{:S(2)}) %all-to-all-start.2) | async-done | bytes 4194336 | tf_op jit(solution)/shard_map/all_to_all | solution.py:11
  165.8 3.1 %multiply_reduce_fusion = f32[2048]{0:T(1024)S(1)} fusion(bf16[16,2048,64]{1,2,0:T(8,128)(2,1)} %all-to-all-done.2), kind=kLoop, calls=%fused_computation.12 | loop fusion | flops 6289408 | bytes 4202496 | tf_op jit(solution)/shard_map/reduce_sum | solution.py:161
  168.9 2.9 %fusion.6 = bf16[2048,1024]{0,1:T(8,128)(2,1)S(1)} fusion(f32[1024]{0:T(1024)S(1)} %copy-done.10, bf16[16,2048,64]{1,2,0:T(8,128)(2,1)} %all-to-all-done.2), kind=kLoop, calls=%fused_computation.9 | loop fusion | flops 6291456 | bytes 8392704 | tf_op jit(solution)/shard_map/convert_element_type | solution.py:158
  171.8 5.1 %multiply_convert_fusion = bf16[2048,1024]{0,1:T(8,128)(2,1)S(1)} fusion(bf16[2048,1024]{0,1:T(8,128)(2,1)S(1)} %fusion.6, bf16[1024,1024]{1,0:T(8,128)(2,1)S(1)} %copy-done, f32[2048]{0:T(1024)S(1)} %add_rsqrt_fusion), kind=kOutput, calls=%fused_computation.10 | convolution fusion | flops 4299161600 | bytes 10493952 | tf_op jit(solution)/shard_map/dot_general | solution.py:159
  176.9 5.1 %multiply_convert_fusion.1 = bf16[2048,1024]{0,1:T(8,128)(2,1)S(1)} fusion(bf16[2048,1024]{0,1:T(8,128)(2,1)S(1)} %fusion.6, bf16[1024,1024]{1,0:T(8,128)(2,1)S(1)} %copy-done.14, f32[2048]{0:T(1024)S(1)} %add_rsqrt_fusion), kind=kOutput, calls=%fused_computation.11 | convolution fusion | flops 4299161600 | bytes 10493952 | tf_op jit(solution)/shard_map/dot_general | solution.py:160
  182.0 10.9 %fusion = (f32[8,384]{1,0:T(8,128)S(1)}, f32[8,384,2048]{2,1,0:T(8,128)}) fusion(pred[384,2048]{1,0:T(8,128)(4,1)S(1)} %copy.102, bf16[2048,8,128]{0,2,1:T(8,128)(2,1)S(1)} %bitcast.76, bf16[48,8,8,128]{3,2,1,0:T(8,128)(2,1)S(1)} %copy-done.4), kind=kOutput, calls=%fused_computation.2 | convolution fusion | flops 1629484032 | bytes 30945280 | tf_op jit(solution)/shard_map/qhd,khd->hqk/dot_general | solution.py:54
  192.9 11.6 %fusion.1 = f32[8,384]{1,0:T(8,128)S(1)} fusion(f32[8,384,2048]{2,1,0:T(8,128)} %get-tuple-element.35, f32[8,384]{1,0:T(8,128)S(1)} %get-tuple-element.34, pred[384,2048]{1,0:T(8,128)(4,1)S(1)} %copy.102), kind=kLoop, calls=%fused_computation.3 | loop fusion | flops 25162752 | bytes 25976832 | tf_op jit(solution)/shard_map/reduce_sum | solution.py:60
  204.5 12.0 %fusion.25 = bf16[384,8,128]{0,2,1:T(8,128)(2,1)S(1)} fusion(bf16[2048,8,128]{0,2,1:T(8,128)(2,1)S(1)} %bitcast.84, f32[8,384,2048]{2,1,0:T(8,128)} %get-tuple-element.35, f32[8,384]{1,0:T(8,128)S(1)} %get-tuple-element.34, pred[384,2048]{1,0:T(8,128)(4,1)S(1)} %copy.102, f32[384,8]{0,1:T(8,128)S(1)} %bitcast.83), kind=kOutput, calls=%fused_computation.38 | convolution fusion | flops 1636564992 | bytes 30957568 | tf_op jit(solution)/shard_map/hqk,khd->qhd/dot_general | solution.py:62
  216.6 1.9 convolution_convert_fusion.4
  218.4 5.0 %all-to-all-start.4 = ((bf16[16,24,1024]{2,1,0:T(8,128)(2,1)}), bf16[16,24,1024]{2,1,0:T(8,128)(2,1)S(1)}, u32[]{:S(2)}, u32[]{:S(2)}) async-start(bf16[16,24,1024]{2,1,0:T(8,128)(2,1)} %bitcast.20), calls=%async_computation.4 | async-start | bytes 1572864 | tf_op jit(solution)/shard_map/all_to_all | solution.py:34
  223.5 13.5 %all-to-all-done.4 = bf16[16,24,1024]{2,1,0:T(8,128)(2,1)S(1)} async-done(((bf16[16,24,1024]{2,1,0:T(8,128)(2,1)}), bf16[16,24,1024]{2,1,0:T(8,128)(2,1)S(1)}, u32[]{:S(2)}, u32[]{:S(2)}) %all-to-all-start.4) | async-done | bytes 786464 | tf_op jit(solution)/shard_map/all_to_all | solution.py:34
  (69 shorter events, 10.2 us)
Async XLA Ops:
  0.6 171.2 %copy-start = (bf16[1024,1024]{1,0:T(8,128)(2,1)S(1)}, bf16[1024,1024]{1,0:T(8,128)(2,1)}, u32[]{:S(2)}) copy-start(bf16[1024,1024]{1,0:T(8,128)(2,1)} %param.31) | copy-start | bytes 6291460
  5.1 4.4 %copy-start.5 = (bf16[512,1024]{1,0:T(8,128)(2,1)S(1)}, bf16[512,1024]{1,0:T(8,128)(2,1)}, u32[]{:S(2)}) copy-start(bf16[512,1024]{1,0:T(8,128)(2,1)} %param.17) | copy-start | bytes 3145732
  5.1 4.4 %copy-start.12 = (bf16[1024,1024]{1,0:T(8,128)(2,1)S(1)}, bf16[1024,1024]{1,0:T(8,128)(2,1)}, u32[]{:S(2)}) copy-start(bf16[1024,1024]{1,0:T(8,128)(2,1)} %param.23) | copy-start | bytes 6291460
  5.1 4.4 %copy-start.15 = (f32[1024]{0:T(1024)S(1)}, f32[1024]{0:T(1024)}, u32[]{:S(2)}) copy-start(f32[1024]{0:T(1024)} %param.21) | copy-start | bytes 12292
  9.5 2.3 copy-start.13
  23.8 1.8 copy-start.6
  25.5 2.6 %copy-start.3 = (bf16[1024,1024]{0,1:T(8,128)(2,1)S(1)}, bf16[1024,1024]{0,1:T(8,128)(2,1)}, u32[]{:S(2)}) copy-start(bf16[1024,1024]{0,1:T(8,128)(2,1)} %copy.92) | copy-start | bytes 6291460
  30.7 7.7 %copy-start.9 = (s32[4]{0:T(128)S(1)}, s32[4]{0:T(128)}, u32[]{:S(2)}) copy-start(s32[4]{0:T(128)} %param.18) | copy-start | bytes 52
  30.7 39.2 %all-to-all-start = ((f32[16,512,64]{1,2,0:T(8,128)}), f32[16,512,64]{1,2,0:T(8,128)}, u32[]{:S(2)}, u32[]{:S(2)}) async-start(f32[16,512,64]{1,2,0:T(8,128)} %convolution_bitcast_fusion), calls=%async_computation | async-start | bytes 4194304 | tf_op jit(solution)/shard_map/all_to_all | solution.py:28
  71.6 26.0 %copy-start.8 = (bf16[512,64]{0,1:T(8,128)(2,1)}, bf16[512,64]{0,1:T(8,128)(2,1)S(1)}, u32[]{:S(2)}) copy-start(bf16[512,64]{0,1:T(8,128)(2,1)S(1)} %add_convert_fusion) | copy-start | bytes 196612
  73.7 12.8 %all-to-all-start.1 = ((bf16[8,2,128,64]{2,3,1,0:T(8,128)(2,1)}), bf16[8,2,128,64]{2,3,1,0:T(8,128)(2,1)S(1)}, u32[]{:S(2)}, u32[]{:S(2)}) async-start(bf16[8,2,128,64]{2,3,1,0:T(8,128)(2,1)} %copy.95), calls=%async_computation.1 | async-start | bytes 524288 | tf_op jit(solution)/shard_map/all_to_all | solution.py:147
  86.6 8.6 %all-to-all-start.3 = ((s32[8,2,2]{1,2,0:T(2,128)}), s32[8,2,2]{1,2,0:T(2,128)S(1)}, u32[]{:S(2)}, u32[]{:S(2)}) async-start(s32[8,2,2]{1,2,0:T(2,128)} %copy.97), calls=%async_computation.3 | async-start | bytes 16384 | tf_op jit(solution)/shard_map/all_to_all | solution.py:154
  97.6 4.7 %copy-start.7 = (bf16[384,1024]{1,0:T(8,128)(2,1)S(1)}, bf16[384,1024]{1,0:T(8,128)(2,1)}, u32[]{:S(2)}) copy-start(bf16[384,1024]{1,0:T(8,128)(2,1)} %param.26) | copy-start | bytes 2359300
  97.6 4.9 %copy-start.16 = (f32[1024]{0:T(1024)S(1)}, f32[1024]{0:T(1024)}, u32[]{:S(2)}) copy-start(f32[1024]{0:T(1024)} %param.28) | copy-start | bytes 12292
  97.6 68.1 %all-to-all-start.2 = ((bf16[16,2048,64]{1,2,0:T(8,128)(2,1)}), bf16[16,2048,64]{1,2,0:T(8,128)(2,1)}, u32[]{:S(2)}, u32[]{:S(2)}) async-start(bf16[16,2048,64]{1,2,0:T(8,128)(2,1)} %stack.10), calls=%async_computation.2 | async-start | bytes 8388608 | tf_op jit(solution)/shard_map/all_to_all | solution.py:11
  102.3 3.9 %copy-start.11 = (s32[384]{0:T(512)S(1)}, s32[384]{0:T(512)}, u32[]{:S(2)}) copy-start(s32[384]{0:T(512)} %param.27) | copy-start | bytes 4612
  106.1 62.7 %copy-start.10 = (f32[1024]{0:T(1024)S(1)}, f32[1024]{0:T(1024)}, u32[]{:S(2)}) copy-start(f32[1024]{0:T(1024)} %param.29) | copy-start | bytes 12292
  171.8 5.1 %copy-start.14 = (bf16[1024,1024]{1,0:T(8,128)(2,1)S(1)}, bf16[1024,1024]{1,0:T(8,128)(2,1)}, u32[]{:S(2)}) copy-start(bf16[1024,1024]{1,0:T(8,128)(2,1)} %param.32) | copy-start | bytes 6291460
  176.9 5.1 %copy-start.4 = (bf16[48,8,8,128]{3,2,1,0:T(8,128)(2,1)S(1)}, bf16[48,8,8,128]{3,2,1,0:T(8,128)(2,1)}, u32[]{:S(2)}) copy-start(bf16[48,8,8,128]{3,2,1,0:T(8,128)(2,1)} %fusion.30) | copy-start | bytes 2359300
  204.5 12.1 %copy-start.2 = (bf16[1024,1024]{1,0:T(8,128)(2,1)S(1)}, bf16[1024,1024]{1,0:T(8,128)(2,1)}, u32[]{:S(2)}) copy-start(bf16[1024,1024]{1,0:T(8,128)(2,1)} %param.33) | copy-start | bytes 6291460
  204.5 34.1 %copy-start.1 = (bf16[1024,1024]{1,0:T(8,128)(2,1)S(1)}, bf16[1024,1024]{1,0:T(8,128)(2,1)}, u32[]{:S(2)}) copy-start(bf16[1024,1024]{1,0:T(8,128)(2,1)} %param.31) | copy-start | bytes 6291460
  218.4 18.5 %all-to-all-start.4 = ((bf16[16,24,1024]{2,1,0:T(8,128)(2,1)}), bf16[16,24,1024]{2,1,0:T(8,128)(2,1)S(1)}, u32[]{:S(2)}, u32[]{:S(2)}) async-start(bf16[16,24,1024]{2,1,0:T(8,128)(2,1)} %bitcast.20), calls=%async_computation.4 | async-start | bytes 1572864 | tf_op jit(solution)/shard_map/all_to_all | solution.py:34
